TPU v7x, 256 devices: a whole 4x4x8 slice. The times are simulated.
256 devices in a mesh: group: 8 (over z), row: 32 (over y, x, core).
Axes of the slice: x: 4, y: 4, z: 8, core: 2. Of those that a mesh axis runs over, the one named last changes fastest.
Arguments:
- start_basis: float32 [2048, 16, 128], P(('group', 'row')), may hold values from -6 to 6
- tiles: bfloat16 [2048, 16, 128, 128], P(('group', 'row')), may hold values from -60000 to 60000
- tile_cols: int32 [2048, 16], P(('group', 'row')), may hold values from 0 to 75, as said below
- tile_count: int32 [2048], P(('group', 'row')), may hold values from 10 to 16, as said below
- recv_list: int32 [8, 32, 32, 2], P('group', 'row'), may hold values from -1 to 2047, as said below
Outputs:
- krylov: float32 [3, 2048, 16, 128], P(None, ('group', 'row'))
Inputs may be any that keep to these rules, and one draw needn't show every extreme that they name: For each reader device and each other device of its range, recv_list names distinct blocks of that peer in its first slots and -1 in the rest; a reader's own entry is all -1; every reader gets exactly 2 blocks from some peer. tile_cols never names an empty receive slot, nor a rim slot of a range that does not exist (before the first or after the last group); every filled receive slot and every existing rim slot is named by some tile slot below 10. `tile_count`: every device has a row block with all 16 tiles live.
All inputs are finite; a program needn't handle non-finite values.
Results may differ from a plain program's by a relative error of at most 0.0003.
Values sent between devices are 32-bit elements; how exact they have to be, the bound alone decides.
A program may use at most 64 MiB of HBM per device.

v0:
```python
import jax
import jax.numpy as jnp
from jax import lax
from jax.sharding import PartitionSpec as P

SLOTS = 2
RIM = 2
ITERS = 3


def padded(x, sides, width):
    for axis, dim in sides:
        count, length = (lax.axis_size(axis), x.shape[dim])
        up = [(i, (i + 1) % count) for i in range(count - 1)]
        down = [(j, i) for i, j in up]
        last = lax.slice_in_dim(x, length - width, length, axis=dim)
        leading = lax.slice_in_dim(x, 0, width, axis=dim)
        before = lax.ppermute(last, axis, up)
        after = lax.ppermute(leading, axis, down)
        x = jnp.concatenate([before, x, after], axis=dim)
    return x


def orthonormal(applied, gram_sum, row_total):
    vectors = applied.shape[1]
    factor = jnp.linalg.cholesky(gram_sum / row_total)
    inverse = lax.linalg.triangular_solve(
        factor, jnp.eye(vectors, dtype=jnp.float32), left_side=True, lower=True
    )
    return jnp.einsum("kl,bli->bki", inverse, applied, precision=lax.Precision.HIGHEST)


def local(start_basis, tiles, tile_cols, tile_count, recv_list):
    groups = lax.axis_size("group")
    peers = lax.axis_size("row")
    group_at = lax.axis_index("group")
    blocks = tiles.shape[0]
    per_row = tiles.shape[1]
    tile_side = tiles.shape[2]
    row_total = groups * peers * blocks * tile_side
    live_mask = (jnp.arange(per_row, dtype=jnp.int32)[None, :] < tile_count[:, None]).astype(
        jnp.float32
    )
    wide_tiles = tiles.astype(jnp.float32)
    sum_sq = jnp.einsum(
        "btij,bt->bi", wide_tiles * wide_tiles, live_mask, precision=lax.Precision.HIGHEST
    )
    inv_root = (1e-06 + sum_sq) ** (-0.25)
    wanted = recv_list.reshape(peers, SLOTS)
    gather_pick = jnp.clip(wanted - group_at * peers * blocks, 0, peers * blocks - 1).reshape(-1)
    results = []
    basis = start_basis
    for step_at in range(ITERS):
        scaled = basis * inv_root[:, None, :]
        rimmed = padded(scaled, (("group", 0),), RIM)
        group_all = lax.all_gather(scaled, "row", axis=0, tiled=True)
        received = jnp.take(group_all, gather_pick, axis=0)
        extended = jnp.concatenate([scaled, received, rimmed[:RIM], rimmed[blocks + RIM :]], axis=0)
        picked = jnp.take(extended, tile_cols, axis=0) * live_mask[:, :, None, None]
        product = jnp.einsum(
            "btij,btkj->bki",
            tiles,
            picked,
            precision=lax.Precision.HIGHEST,
            preferred_element_type=jnp.float32,
        )
        applied = product * inv_root[:, None, :]
        partial_value = jnp.einsum("bki,bli->kl", applied, applied, precision=lax.Precision.HIGHEST)
        gram_sum = lax.psum(partial_value, ("group", "row"))
        basis = orthonormal(applied, gram_sum, row_total)
        results.append(basis)
    return jnp.stack(results)


def solution(mesh):
    placed = (
        P(("group", "row"), None, None),
        P(("group", "row"), None, None, None),
        P(("group", "row"), None),
        P(("group", "row")),
        P("group", "row", None, None),
    )
    return jax.shard_map(
        local,
        mesh=mesh,
        in_specs=placed,
        out_specs=P(None, ("group", "row"), None, None),
        check_vma=False,
    )
```

profile of v0, /device:TPU:1, one launch (start us, length us, event | category | flops | bytes accessed | tf_op | source)
XLA Modules:
  0.0 434.7 jit_solution(10057653734697218750)
XLA Ops:
  6.6 4.5 %multiply_reduce_fusion = f32[8,16,128]{2,1,0:T(8,128)S(1)} fusion(bf16[8,16,128,128]{3,2,1,0:T(8,128)(2,1)} %param.13), kind=kLoop, calls=%fused_computation.6 | loop fusion | flops 6275072 | bytes 4259840 | tf_op jit(solution)/shard_map/btij,bt->bi/reduce_sum | solution.py:45
  12.8 4.4 %collective-permute-start = (f32[2,16,128]{2,1,0:T(8,128)S(1)}, f32[2,16,128]{2,1,0:T(8,128)S(1)}, u32[]{:S(2)}, u32[]{:S(2)}) collective-permute-start(f32[2,16,128]{2,1,0:T(8,128)S(1)} %get-tuple-element.13), channel_id=1, source_target_pairs={{0,32},{32,64},{64,96},{96,128},{128,160},{160,192},{192,224},{1,3... | collective-permute-start | bytes 49160 | tf_op jit(solution)/shard_map/ppermute | solution.py:18
  17.2 1.3 collective-permute-start.1
  18.8 46.4 %all-gather.4.cloned.1.call-done = f32[256,16,128]{2,1,0:T(8,128)} async-done(((f32[8,16,128]{2,1,0:T(8,128)}), f32[256,16,128]{2,1,0:T(8,128)}) %all-gather.4.cloned.1.call-update) | async-done | bytes 2097168 | tf_op jit(solution)/shard_map/all_gather | solution.py:56
  65.2 2.2 gather_fusion
  67.6 0.9 pad_maximum_fusion
  68.5 0.8 gather_fusion.1
  69.2 5.2 %fusion.2 = f32[8,16,128]{2,1,0:T(8,128)S(1)} fusion(bf16[8,16,128,128]{3,2,1,0:T(8,128)(2,1)} %param.13, f32[8,16,16,128]{3,2,1,0:T(8,128)S(1)} %bitcast.92, f32[8,16]{1,0:T(8,128)S(1)} %get-tuple-element.15, pred[8,16]{1,0:T(8,128)(4,1)S(1)} %get-tuple-element.21, f32[8,128]{1,0:T(8,128)S(1)} %add_power_fusion), kind=kOutput, calls=%fused_computation.13 | convolution fusion | flops 403193856 | bytes 5313152 | tf_op jit(solution)/shard_map/btij,btkj->bki/dot_general | solution.py:60
  74.6 75.6 %psum.21 = f32[16,16]{0,1:T(8,128)S(1)} all-reduce(f32[16,16]{0,1:T(8,128)S(1)} %convolution_bitcast_fusion.9), channel_id=1, replica_groups=mesh['group'=8,'row'=32] {'group','row'}, use_global_device_ids=true, to_apply=%region_1.0 | all-reduce | flops 256 | bytes 2048 | tf_op jit(solution)/shard_map/psum | solution.py:69
  150.3 1.5 cholesky.59
  153.0 1.2 custom-call.7
  154.5 0.8 bitcast_multiply_fusion.1
  156.1 2.9 collective-permute-start.2
  159.1 1.3 collective-permute-start.3
  160.4 41.2 %all-gather.6.cloned.1.call-done = f32[256,16,128]{2,1,0:T(8,128)} async-done(((f32[8,16,128]{2,1,0:T(8,128)}), f32[256,16,128]{2,1,0:T(8,128)}) %all-gather.6.cloned.1.call-update) | async-done | bytes 2097168 | tf_op jit(solution)/shard_map/all_gather | solution.py:56
  201.6 2.2 gather_fusion.2
  204.0 0.9 pad_maximum_fusion.1
  204.9 0.8 gather_fusion.3
  205.6 5.2 %fusion.1 = f32[8,16,128]{2,1,0:T(8,128)S(1)} fusion(bf16[8,16,128,128]{3,2,1,0:T(8,128)(2,1)} %param.13, f32[8,16,16,128]{3,2,1,0:T(8,128)S(1)} %bitcast.93, f32[8,16]{1,0:T(8,128)S(1)} %get-tuple-element.15, pred[8,16]{1,0:T(8,128)(4,1)S(1)} %get-tuple-element.21, f32[8,128]{1,0:T(8,128)S(1)} %add_power_fusion), kind=kOutput, calls=%fused_computation.11 | convolution fusion | flops 403193856 | bytes 5313152 | tf_op jit(solution)/shard_map/btij,btkj->bki/dot_general | solution.py:60
  211.0 75.6 %psum.22 = f32[16,16]{0,1:T(8,128)S(1)} all-reduce(f32[16,16]{0,1:T(8,128)S(1)} %convolution_bitcast_fusion.7), channel_id=1, replica_groups=mesh['group'=8,'row'=32] {'group','row'}, use_global_device_ids=true, to_apply=%region_4.9 | all-reduce | flops 256 | bytes 2048 | tf_op jit(solution)/shard_map/psum | solution.py:69
  286.6 1.5 cholesky.70
  289.4 1.2 custom-call.8
  290.9 0.8 bitcast_multiply_fusion
  292.5 2.9 collective-permute-start.4
  295.4 1.3 collective-permute-start.5
  296.7 41.3 %all-gather.8.cloned.1.call-done = f32[256,16,128]{2,1,0:T(8,128)} async-done(((f32[8,16,128]{2,1,0:T(8,128)}), f32[256,16,128]{2,1,0:T(8,128)}) %all-gather.8.cloned.1.call-update) | async-done | bytes 2097168 | tf_op jit(solution)/shard_map/all_gather | solution.py:56
  338.0 2.2 gather_fusion.4
  340.4 0.9 pad_maximum_fusion.2
  342.0 5.2 %fusion = f32[8,16,128]{2,1,0:T(8,128)S(1)} fusion(bf16[8,16,128,128]{3,2,1,0:T(8,128)(2,1)} %param.13, f32[8,16,16,128]{3,2,1,0:T(8,128)S(1)} %bitcast.91, f32[8,16]{1,0:T(8,128)S(1)} %get-tuple-element.15, pred[8,16]{1,0:T(8,128)(4,1)S(1)} %get-tuple-element.21, f32[8,128]{1,0:T(8,128)S(1)} %add_power_fusion), kind=kOutput, calls=%fused_computation.9 | convolution fusion | flops 403193856 | bytes 5313152 | tf_op jit(solution)/shard_map/btij,btkj->bki/dot_general | solution.py:60
  347.4 75.6 %psum.23 = f32[16,16]{0,1:T(8,128)S(1)} all-reduce(f32[16,16]{0,1:T(8,128)S(1)} %convolution_bitcast_fusion.5), channel_id=1, replica_groups=mesh['group'=8,'row'=32] {'group','row'}, use_global_device_ids=true, to_apply=%region_5.10 | all-reduce | flops 256 | bytes 2048 | tf_op jit(solution)/shard_map/psum | solution.py:69
  423.0 1.5 cholesky.81
  425.8 1.2 custom-call.9
  (66 shorter events, 11.1 us)
Async XLA Ops:
  6.5 4.5 %copy-start.1 = (s32[8,16]{1,0:T(8,128)S(1)}, s32[8,16]{1,0:T(8,128)}, u32[]{:S(2)}) copy-start(s32[8,16]{1,0:T(8,128)} %param.14) | copy-start | bytes 1540
  6.5 4.5 %copy-start.3 = (s32[8]{0:T(128)S(1)}, s32[8]{0:T(128)}, u32[]{:S(2)}) copy-start(s32[8]{0:T(128)} %param.15) | copy-start | bytes 100
  6.5 4.8 %copy-start = (f32[8,16,128]{2,1,0:T(8,128)S(1)}, f32[8,16,128]{2,1,0:T(8,128)}, u32[]{:S(2)}) copy-start(f32[8,16,128]{2,1,0:T(8,128)} %param.12) | copy-start | bytes 196612
  6.5 12.0 %copy-start.2 = (s32[1,1,32,2]{2,3,1,0:T(2,128)S(1)}, s32[1,1,32,2]{2,3,1,0:T(2,128)}, u32[]{:S(2)}) copy-start(s32[1,1,32,2]{2,3,1,0:T(2,128)} %param.16) | copy-start | bytes 772
  6.5 58.7 %all-gather.4.cloned.1.call-start = ((), (), s32[]{:S(2)}) async-start(), calls=%async_computation | async-start | bytes 2162688 | tf_op jit(solution)/shard_map/all_gather | solution.py:56
  12.0 189.6 %all-gather.6.cloned.1.call-start = ((), (), s32[]{:S(2)}) async-start(), calls=%async_computation.1 | async-start | bytes 2162688 | tf_op jit(solution)/shard_map/all_gather | solution.py:56
  12.8 54.8 %collective-permute-start = (f32[2,16,128]{2,1,0:T(8,128)S(1)}, f32[2,16,128]{2,1,0:T(8,128)S(1)}, u32[]{:S(2)}, u32[]{:S(2)}) collective-permute-start(f32[2,16,128]{2,1,0:T(8,128)S(1)} %get-tuple-element.13), channel_id=1, source_target_pairs={{0,32},{32,64},{64,96},{96,128},{128,160},{160,192},{192,224},{1,3... | collective-permute-start | bytes 49160 | tf_op jit(solution)/shard_map/ppermute | solution.py:18
  17.2 50.4 %collective-permute-start.1 = (f32[2,16,128]{2,1,0:T(8,128)S(1)}, f32[2,16,128]{2,1,0:T(8,128)S(1)}, u32[]{:S(2)}, u32[]{:S(2)}) collective-permute-start(f32[2,16,128]{2,1,0:T(8,128)S(1)} %get-tuple-element.14), channel_id=1, source_target_pairs={{32,0},{64,32},{96,64},{128,96},{160,128},{192,160},{224,192},{33,... | collective-permute-start | bytes 49160 | tf_op jit(solution)/shard_map/ppermute | solution.py:19
  155.3 182.7 %all-gather.8.cloned.1.call-start = ((), (), s32[]{:S(2)}) async-start(), calls=%async_computation.2 | async-start | bytes 2162688 | tf_op jit(solution)/shard_map/all_gather | solution.py:56
  156.1 47.8 %collective-permute-start.2 = (f32[2,16,128]{2,1,0:T(8,128)S(1)}, f32[2,16,128]{2,1,0:T(8,128)S(1)}, u32[]{:S(2)}, u32[]{:S(2)}) collective-permute-start(f32[2,16,128]{2,1,0:T(8,128)S(1)} %get-tuple-element.10), channel_id=1, source_target_pairs={{0,32},{32,64},{64,96},{96,128},{128,160},{160,192},{192,224},{1,3... | collective-permute-start | bytes 49160 | tf_op jit(solution)/shard_map/ppermute | solution.py:18
  159.1 44.9 %collective-permute-start.3 = (f32[2,16,128]{2,1,0:T(8,128)S(1)}, f32[2,16,128]{2,1,0:T(8,128)S(1)}, u32[]{:S(2)}, u32[]{:S(2)}) collective-permute-start(f32[2,16,128]{2,1,0:T(8,128)S(1)} %get-tuple-element.12), channel_id=1, source_target_pairs={{32,0},{64,32},{96,64},{128,96},{160,128},{192,160},{224,192},{33,... | collective-permute-start | bytes 49160 | tf_op jit(solution)/shard_map/ppermute | solution.py:19
  292.5 47.9 %collective-permute-start.4 = (f32[2,16,128]{2,1,0:T(8,128)S(1)}, f32[2,16,128]{2,1,0:T(8,128)S(1)}, u32[]{:S(2)}, u32[]{:S(2)}) collective-permute-start(f32[2,16,128]{2,1,0:T(8,128)S(1)} %get-tuple-element.6), channel_id=1, source_target_pairs={{0,32},{32,64},{64,96},{96,128},{128,160},{160,192},{192,224},{1,3... | collective-permute-start | bytes 49160 | tf_op jit(solution)/shard_map/ppermute | solution.py:18
  295.4 44.9 %collective-permute-start.5 = (f32[2,16,128]{2,1,0:T(8,128)S(1)}, f32[2,16,128]{2,1,0:T(8,128)S(1)}, u32[]{:S(2)}, u32[]{:S(2)}) collective-permute-start(f32[2,16,128]{2,1,0:T(8,128)S(1)} %get-tuple-element.8), channel_id=1, source_target_pairs={{32,0},{64,32},{96,64},{128,96},{160,128},{192,160},{224,192},{33,... | collective-permute-start | bytes 49160 | tf_op jit(solution)/shard_map/ppermute | solution.py:19
Sparse Core Ops, SparseCore 0:
  12.1 53.0 all-gather.3
  155.5 46.1 all-gather.5
  291.8 46.1 all-gather.7
where the time goes:
time: 436 us; the launch traced here: 435 us
  blocking collectives  227 us (52%)
  waiting for transfers between devices  129 us (30%)
  other arithmetic  21 us (5%)
  matrix products  18.7 us (4%)
  starting transfers between devices  14.2 us (3%)
  between operations  13.4 us (3%)
  local copies, waits for them, and re-layouts  11.6 us (3%)
    psum x3, blocking collectives, local(): gram_sum = lax.psum(partial_value, ('group', 'row'))  227 us
    all_gather x3, waiting for transfers between devices, local(): group_all = lax.all_gather(scaled, 'row', axis=0, tiled=True)  129 us
    dot_general x3, matrix products, local(): jnp.einsum('btij,btkj->bki', tiles, picked, precision=lax.Precision.HIGHE...  15.5 us
    ppermute x3, starting transfers between devices, padded(): before = lax.ppermute(last, axis, up)  10.2 us
  transfers between devices with their start and end apart: 9, of which 3 were waited for; matrix products, arithmetic and copies ran while one was open for 2% of the time, Pallas kernels for 0%

commit v1 on v0

--- a/solution.py
+++ b/solution.py
@@ -53,7 +53,17 @@
     for step_at in range(ITERS):
         scaled = basis * inv_root[:, None, :]
         rimmed = padded(scaled, (("group", 0),), RIM)
-        group_all = lax.all_gather(scaled, "row", axis=0, tiled=True)
+
+        def return_all_the_squares(patch):
+            local_out = jax.lax.all_to_all(
+                jnp.stack([patch] * jax.lax.axis_size("row"), axis=0),
+                split_axis=0,
+                axis_name="row",
+                concat_axis=0,
+            )
+            return jnp.concatenate(local_out, axis=0)
+
+        group_all = return_all_the_squares(scaled)
         received = jnp.take(group_all, gather_pick, axis=0)
         extended = jnp.concatenate([scaled, received, rimmed[:RIM], rimmed[blocks + RIM :]], axis=0)
         picked = jnp.take(extended, tile_cols, axis=0) * live_mask[:, :, None, None]

time: 436 us -> 376 us (0.86)
  waiting for transfers between devices: 129 us -> 69.4 us
  starting transfers between devices: 14.2 us -> 31.2 us
  between operations: 13.4 us -> 0.42 us
    all_gather x3 -> x0, waiting for transfers between devices: 129 us -> none  [local(): group_all = lax.all_gather(scaled, 'row', axis=0, tiled=True)]
    all_to_all x0 -> x3, waiting for transfers between devices: none -> 69.4 us  [return_all_the_squares(): jax.lax.all_to_all(jnp.stack([patch] * jax.lax.axis_size('row'), axis=0),...]
    all_to_all x0 -> x3, starting transfers between devices: none -> 17.3 us  [return_all_the_squares(): jax.lax.all_to_all(jnp.stack([patch] * jax.lax.axis_size('row'), axis=0),...]
    another operation x0 -> x3, local copies, waits for them, and re-layouts: none -> 4.77 us  [return_all_the_squares(): jnp.stack([patch] * jax.lax.axis_size('row'), axis=0)]
    gather x3, local copies, waits for them, and re-layouts: 6.55 us -> 1.89 us  [local(): received = jnp.take(group_all, gather_pick, axis=0)]
  transfers between devices with their start and end apart: 9 -> 9, of which waited for: 3 -> 3; matrix products, arithmetic and copies ran while one was open for 2% -> 1% of each run, Pallas kernels for 0% -> 0%
where the time goes in v1:
time: 376 us; the launch traced here: 375 us
  blocking collectives  229 us (61%)
  waiting for transfers between devices  69.4 us (18%)
  starting transfers between devices  31.2 us (8%)
  other arithmetic  17.9 us (5%)
  matrix products  17.5 us (5%)
  local copies, waits for them, and re-layouts  9.45 us (3%)
    psum x3, blocking collectives, local(): gram_sum = lax.psum(partial_value, ('group', 'row'))  229 us
    all_to_all x3, waiting for transfers between devices, return_all_the_squares(): jax.lax.all_to_all(jnp.stack([patch] * jax.lax.axis_size('row'), axis=0),...  69.4 us
    all_to_all x3, starting transfers between devices, return_all_the_squares(): jax.lax.all_to_all(jnp.stack([patch] * jax.lax.axis_size('row'), axis=0),...  17.3 us
    dot_general x3, matrix products, local(): jnp.einsum('btij,btkj->bki', tiles, picked, precision=lax.Precision.HIGHE...  15.5 us
    ppermute x3, starting transfers between devices, padded(): before = lax.ppermute(last, axis, up)  9.86 us
  transfers between devices with their start and end apart: 9, of which 3 were waited for; matrix products, arithmetic and copies ran while one was open for 1% of the time, Pallas kernels for 0%

profile of v1, /device:TPU:1, one launch (start us, length us, event | category | flops | bytes accessed | tf_op | source)
XLA Modules:
  0.0 374.8 jit_solution(9229263293565618943)
XLA Ops:
  0.0 4.5 %multiply_reduce_fusion = f32[8,16,128]{2,1,0:T(8,128)S(1)} fusion(bf16[8,16,128,128]{3,2,1,0:T(8,128)(2,1)} %param.13), kind=kLoop, calls=%fused_computation.6 | loop fusion | flops 6275072 | bytes 4259840 | tf_op jit(solution)/shard_map/btij,bt->bi/reduce_sum | solution.py:45
  4.8 1.6 stack.14
  6.4 8.6 %all-to-all-start = ((f32[32,8,16,128]{3,2,1,0:T(8,128)}), f32[32,8,16,128]{3,2,1,0:T(8,128)S(1)}, u32[]{:S(2)}, u32[]{:S(2)}) async-start(f32[32,8,16,128]{3,2,1,0:T(8,128)} %stack.14), calls=%async_computation | async-start | bytes 4194304 | tf_op jit(solution)/shard_map/all_to_all | solution.py:58
  15.0 3.5 collective-permute-start
  18.5 1.3 collective-permute-start.1
  20.2 22.6 %all-to-all-done = f32[32,8,16,128]{3,2,1,0:T(8,128)S(1)} async-done(((f32[32,8,16,128]{3,2,1,0:T(8,128)}), f32[32,8,16,128]{3,2,1,0:T(8,128)S(1)}, u32[]{:S(2)}, u32[]{:S(2)}) %all-to-all-start) | async-done | bytes 2097184 | tf_op jit(solution)/shard_map/all_to_all | solution.py:58
  43.7 0.8 gather_fusion.1
  44.4 5.2 %fusion.2 = f32[8,16,128]{2,1,0:T(8,128)S(1)} fusion(bf16[8,16,128,128]{3,2,1,0:T(8,128)(2,1)} %param.13, f32[8,16,16,128]{3,2,1,0:T(8,128)S(1)} %bitcast.95, f32[8,16]{1,0:T(8,128)S(1)} %get-tuple-element.15, pred[8,16]{1,0:T(8,128)(4,1)S(1)} %get-tuple-element.21, f32[8,128]{1,0:T(8,128)S(1)} %add_power_fusion), kind=kOutput, calls=%fused_computation.13 | convolution fusion | flops 403193856 | bytes 5313152 | tf_op jit(solution)/shard_map/btij,btkj->bki/dot_general | solution.py:70
  49.8 79.3 %psum.21 = f32[16,16]{0,1:T(8,128)S(1)} all-reduce(f32[16,16]{0,1:T(8,128)S(1)} %convolution_bitcast_fusion.9), channel_id=1, replica_groups=mesh['group'=8,'row'=32] {'group','row'}, use_global_device_ids=true, to_apply=%region_1.0 | all-reduce | flops 256 | bytes 2048 | tf_op jit(solution)/shard_map/psum | solution.py:79
  129.2 1.5 cholesky.59
  132.0 1.2 custom-call.7
  133.6 1.6 stack.16
  135.2 4.3 %all-to-all-start.1 = ((f32[32,8,16,128]{3,2,1,0:T(8,128)}), f32[32,8,16,128]{3,2,1,0:T(8,128)S(1)}, u32[]{:S(2)}, u32[]{:S(2)}) async-start(f32[32,8,16,128]{3,2,1,0:T(8,128)} %stack.16), calls=%async_computation.1 | async-start | bytes 4194304 | tf_op jit(solution)/shard_map/all_to_all | solution.py:58
  139.6 2.6 collective-permute-start.2
  142.2 1.3 collective-permute-start.3
  143.5 24.0 %all-to-all-done.1 = f32[32,8,16,128]{3,2,1,0:T(8,128)S(1)} async-done(((f32[32,8,16,128]{3,2,1,0:T(8,128)}), f32[32,8,16,128]{3,2,1,0:T(8,128)S(1)}, u32[]{:S(2)}, u32[]{:S(2)}) %all-to-all-start.1) | async-done | bytes 2097184 | tf_op jit(solution)/shard_map/all_to_all | solution.py:58
  168.4 0.8 gather_fusion.3
  169.1 5.2 %fusion.1 = f32[8,16,128]{2,1,0:T(8,128)S(1)} fusion(bf16[8,16,128,128]{3,2,1,0:T(8,128)(2,1)} %param.13, f32[8,16,16,128]{3,2,1,0:T(8,128)S(1)} %bitcast.96, f32[8,16]{1,0:T(8,128)S(1)} %get-tuple-element.15, pred[8,16]{1,0:T(8,128)(4,1)S(1)} %get-tuple-element.21, f32[8,128]{1,0:T(8,128)S(1)} %add_power_fusion), kind=kOutput, calls=%fused_computation.11 | convolution fusion | flops 403193856 | bytes 5313152 | tf_op jit(solution)/shard_map/btij,btkj->bki/dot_general | solution.py:70
  174.5 74.4 %psum.22 = f32[16,16]{0,1:T(8,128)S(1)} all-reduce(f32[16,16]{0,1:T(8,128)S(1)} %convolution_bitcast_fusion.7), channel_id=1, replica_groups=mesh['group'=8,'row'=32] {'group','row'}, use_global_device_ids=true, to_apply=%region_4.9 | all-reduce | flops 256 | bytes 2048 | tf_op jit(solution)/shard_map/psum | solution.py:79
  249.0 1.5 cholesky.70
  251.8 1.2 custom-call.8
  253.4 1.6 stack.18
  255.0 4.3 %all-to-all-start.2 = ((f32[32,8,16,128]{3,2,1,0:T(8,128)}), f32[32,8,16,128]{3,2,1,0:T(8,128)S(1)}, u32[]{:S(2)}, u32[]{:S(2)}) async-start(f32[32,8,16,128]{3,2,1,0:T(8,128)} %stack.18), calls=%async_computation.2 | async-start | bytes 4194304 | tf_op jit(solution)/shard_map/all_to_all | solution.py:58
  259.4 3.7 collective-permute-start.4
  263.0 1.5 collective-permute-start.5
  264.5 22.8 %all-to-all-done.2 = f32[32,8,16,128]{3,2,1,0:T(8,128)S(1)} async-done(((f32[32,8,16,128]{3,2,1,0:T(8,128)}), f32[32,8,16,128]{3,2,1,0:T(8,128)S(1)}, u32[]{:S(2)}, u32[]{:S(2)}) %all-to-all-start.2) | async-done | bytes 2097184 | tf_op jit(solution)/shard_map/all_to_all | solution.py:58
  288.1 0.8 gather_fusion.5
  288.9 5.2 %fusion = f32[8,16,128]{2,1,0:T(8,128)S(1)} fusion(bf16[8,16,128,128]{3,2,1,0:T(8,128)(2,1)} %param.13, f32[8,16,16,128]{3,2,1,0:T(8,128)S(1)} %bitcast.94, f32[8,16]{1,0:T(8,128)S(1)} %get-tuple-element.15, pred[8,16]{1,0:T(8,128)(4,1)S(1)} %get-tuple-element.21, f32[8,128]{1,0:T(8,128)S(1)} %add_power_fusion), kind=kOutput, calls=%fused_computation.9 | convolution fusion | flops 403193856 | bytes 5313152 | tf_op jit(solution)/shard_map/btij,btkj->bki/dot_general | solution.py:70
  294.3 75.3 %psum.23 = f32[16,16]{0,1:T(8,128)S(1)} all-reduce(f32[16,16]{0,1:T(8,128)S(1)} %convolution_bitcast_fusion.5), channel_id=1, replica_groups=mesh['group'=8,'row'=32] {'group','row'}, use_global_device_ids=true, to_apply=%region_5.10 | all-reduce | flops 256 | bytes 2048 | tf_op jit(solution)/shard_map/psum | solution.py:79
  369.6 1.5 cholesky.81
  372.4 1.2 custom-call.9
  374.1 0.7 pad_maximum_fusion.3
  (66 shorter events, 9.0 us)
Async XLA Ops:
  0.0 4.5 %copy-start.1 = (s32[8,16]{1,0:T(8,128)S(1)}, s32[8,16]{1,0:T(8,128)}, u32[]{:S(2)}) copy-start(s32[8,16]{1,0:T(8,128)} %param.14) | copy-start | bytes 1540
  0.0 4.5 %copy-start.3 = (s32[8]{0:T(128)S(1)}, s32[8]{0:T(128)}, u32[]{:S(2)}) copy-start(s32[8]{0:T(128)} %param.15) | copy-start | bytes 100
  0.0 4.8 %copy-start = (f32[8,16,128]{2,1,0:T(8,128)S(1)}, f32[8,16,128]{2,1,0:T(8,128)}, u32[]{:S(2)}) copy-start(f32[8,16,128]{2,1,0:T(8,128)} %param.12) | copy-start | bytes 196612
  4.5 15.4 %copy-start.2 = (s32[1,1,32,2]{2,3,1,0:T(2,128)S(1)}, s32[1,1,32,2]{2,3,1,0:T(2,128)}, u32[]{:S(2)}) copy-start(s32[1,1,32,2]{2,3,1,0:T(2,128)} %param.16) | copy-start | bytes 772
  6.4 36.4 %all-to-all-start = ((f32[32,8,16,128]{3,2,1,0:T(8,128)}), f32[32,8,16,128]{3,2,1,0:T(8,128)S(1)}, u32[]{:S(2)}, u32[]{:S(2)}) async-start(f32[32,8,16,128]{3,2,1,0:T(8,128)} %stack.14), calls=%async_computation | async-start | bytes 4194304 | tf_op jit(solution)/shard_map/all_to_all | solution.py:58
  15.0 28.6 %collective-permute-start = (f32[2,16,128]{2,1,0:T(8,128)S(1)}, f32[2,16,128]{2,1,0:T(8,128)S(1)}, u32[]{:S(2)}, u32[]{:S(2)}) collective-permute-start(f32[2,16,128]{2,1,0:T(8,128)S(1)} %get-tuple-element.13), channel_id=1, source_target_pairs={{0,32},{32,64},{64,96},{96,128},{128,160},{160,192},{192,224},{1,3... | collective-permute-start | bytes 49160 | tf_op jit(solution)/shard_map/ppermute | solution.py:18
  18.5 25.1 %collective-permute-start.1 = (f32[2,16,128]{2,1,0:T(8,128)S(1)}, f32[2,16,128]{2,1,0:T(8,128)S(1)}, u32[]{:S(2)}, u32[]{:S(2)}) collective-permute-start(f32[2,16,128]{2,1,0:T(8,128)S(1)} %get-tuple-element.14), channel_id=1, source_target_pairs={{32,0},{64,32},{96,64},{128,96},{160,128},{192,160},{224,192},{33,... | collective-permute-start | bytes 49160 | tf_op jit(solution)/shard_map/ppermute | solution.py:19
  135.2 32.3 %all-to-all-start.1 = ((f32[32,8,16,128]{3,2,1,0:T(8,128)}), f32[32,8,16,128]{3,2,1,0:T(8,128)S(1)}, u32[]{:S(2)}, u32[]{:S(2)}) async-start(f32[32,8,16,128]{3,2,1,0:T(8,128)} %stack.16), calls=%async_computation.1 | async-start | bytes 4194304 | tf_op jit(solution)/shard_map/all_to_all | solution.py:58
  139.6 28.7 %collective-permute-start.2 = (f32[2,16,128]{2,1,0:T(8,128)S(1)}, f32[2,16,128]{2,1,0:T(8,128)S(1)}, u32[]{:S(2)}, u32[]{:S(2)}) collective-permute-start(f32[2,16,128]{2,1,0:T(8,128)S(1)} %get-tuple-element.10), channel_id=1, source_target_pairs={{0,32},{32,64},{64,96},{96,128},{128,160},{160,192},{192,224},{1,3... | collective-permute-start | bytes 49160 | tf_op jit(solution)/shard_map/ppermute | solution.py:18
  142.2 26.1 %collective-permute-start.3 = (f32[2,16,128]{2,1,0:T(8,128)S(1)}, f32[2,16,128]{2,1,0:T(8,128)S(1)}, u32[]{:S(2)}, u32[]{:S(2)}) collective-permute-start(f32[2,16,128]{2,1,0:T(8,128)S(1)} %get-tuple-element.12), channel_id=1, source_target_pairs={{32,0},{64,32},{96,64},{128,96},{160,128},{192,160},{224,192},{33,... | collective-permute-start | bytes 49160 | tf_op jit(solution)/shard_map/ppermute | solution.py:19
  255.0 32.3 %all-to-all-start.2 = ((f32[32,8,16,128]{3,2,1,0:T(8,128)}), f32[32,8,16,128]{3,2,1,0:T(8,128)S(1)}, u32[]{:S(2)}, u32[]{:S(2)}) async-start(f32[32,8,16,128]{3,2,1,0:T(8,128)} %stack.18), calls=%async_computation.2 | async-start | bytes 4194304 | tf_op jit(solution)/shard_map/all_to_all | solution.py:58
  259.4 28.7 %collective-permute-start.4 = (f32[2,16,128]{2,1,0:T(8,128)S(1)}, f32[2,16,128]{2,1,0:T(8,128)S(1)}, u32[]{:S(2)}, u32[]{:S(2)}) collective-permute-start(f32[2,16,128]{2,1,0:T(8,128)S(1)} %get-tuple-element.6), channel_id=1, source_target_pairs={{0,32},{32,64},{64,96},{96,128},{128,160},{160,192},{192,224},{1,3... | collective-permute-start | bytes 49160 | tf_op jit(solution)/shard_map/ppermute | solution.py:18
  263.0 25.0 %collective-permute-start.5 = (f32[2,16,128]{2,1,0:T(8,128)S(1)}, f32[2,16,128]{2,1,0:T(8,128)S(1)}, u32[]{:S(2)}, u32[]{:S(2)}) collective-permute-start(f32[2,16,128]{2,1,0:T(8,128)S(1)} %get-tuple-element.8), channel_id=1, source_target_pairs={{32,0},{64,32},{96,64},{128,96},{160,128},{192,160},{224,192},{33,... | collective-permute-start | bytes 49160 | tf_op jit(solution)/shard_map/ppermute | solution.py:19
